TPU v7x, 32 devices: a whole 2x2x4 slice. The times are simulated.
32 devices in a mesh: dp: 8 (over z, y), expert: 4 (over x, core).
Axes of the slice: x: 2, y: 2, z: 4, core: 2. Of those that a mesh axis runs over, the one named last changes fastest.
Arguments:
- tokens: bfloat16 [1024, 4096], P('dp'), may hold values from -6 to 6
- upstream: bfloat16 [1024, 4096], P('dp', 'expert'), may hold values from -6 to 6
- gates: bfloat16 [1024, 2], P('dp'), may hold values from 0.049804688 to 1
- expert_ids: int32 [1024, 2], P('dp'), may hold values from 0 to 7, all different within a row; in each aligned block of 128 rows (0 to 127, 128 to 255, ...) at most 64 rows name the same one
- w_gate: bfloat16 [8, 1536, 4096], P('dp', 'expert'), may hold values from -0.09375 to 0.09375
- w_up: bfloat16 [8, 1536, 4096], P('dp', 'expert'), may hold values from -0.09375 to 0.09375
- w_down: bfloat16 [8, 1536, 4096], P('dp', 'expert'), may hold values from -0.15625 to 0.15625
Outputs:
- grad_x: bfloat16 [1024, 4096], P('dp', 'expert')
- grad_gates: float32 [1024, 2], P('dp')
- grad_w_gate: bfloat16 [8, 1536, 4096], P('dp', 'expert')
- grad_w_up: bfloat16 [8, 1536, 4096], P('dp', 'expert')
- grad_w_down: bfloat16 [8, 1536, 4096], P('dp', 'expert')
Inputs may be any that keep to these rules, and one draw needn't show every extreme that they name: `expert_ids`: each row names 2 different experts. In each aligned block of 128 rows (the tokens of one index of dp) no expert is named by more than 64 rows, a bound that some block reaches.
All inputs are finite; a program needn't handle non-finite values.
Results may differ from a plain program's by a relative error of at most 0.012.
Values may be sent and summed in bfloat16 or wider, within the bound.
A program may use at most 128 MiB of HBM per device.

v0:
```python
import functools

import jax
import jax.numpy as jnp
from jax import lax
from jax.experimental import pallas as pl
from jax.experimental.pallas import tpu as pltpu
from jax.sharding import PartitionSpec as P

MESH = pltpu.DeviceIdType.MESH if hasattr(pltpu, "DeviceIdType") else pl.DeviceIdType.MESH


def contract_last(left, right):
    return lax.dot_general(
        left, right, (((1,), (1,)), ((), ())), preferred_element_type=jnp.float32
    )


def contract_first(left, right):
    return lax.dot_general(
        left, right, (((0,), (0,)), ((), ())), preferred_element_type=jnp.float32
    )


def matmul(left, right):
    return jnp.dot(left, right, preferred_element_type=jnp.float32)


def kernel(
    groups, parts,
    send_t, send_u, send_s, w_g_hbm, w_u_hbm, w_d_hbm,
    home, home_s, out_g, out_u, out_d,
    recv_t, recv_u, recv_s, weights, pre, flipped, straight, grads,
    term, term_recv, total_term,
    pair_send, pair_recv, side_send, side_recv, own_sum, out_send,
    w_sem, g_sem, local_sem, recv_sem, scale_sem, dp_send, pair_fwd, side_fwd,
    scale_send, pair_send_sem, pair_recv_sem, side_send_sem, side_recv_sem,
    home_send, home_recv, term_send, term_sem, back_send, back_recv,
):
    me, own = lax.axis_index("dp"), lax.axis_index("expert")
    core, place = lax.rem(own, 2), lax.div(own, 2)
    places = parts // 2
    partner = place * 2 + (1 - core)
    cap, part = send_t.shape[1:]
    rows = groups * cap
    hid = weights.shape[2]
    sends, recvs = (send_t, send_u), (recv_t, recv_u)

    paired = groups & (groups - 1) == 0

    def crossed(k):
        spot = me
        for bit in [1 << b for b in range(groups.bit_length()) if k >> b & 1]:
            spot = spot + bit * (1 - 2 * lax.rem(lax.div(me, bit), 2))
        return spot

    def ahead(k):
        return crossed(k) if paired else lax.rem(me + k, groups)

    def behind(k):
        return crossed(k) if paired else lax.rem(me + groups - k, groups)

    def aside(j):
        return lax.rem(place + j, places)

    def remote(src, dst, send_sem, sem, target):
        return pltpu.make_async_remote_copy(
            src_ref=src, dst_ref=dst, send_sem=send_sem, recv_sem=sem,
            device_id=target, device_id_type=MESH,
        )

    def arrived(ref, sem):
        pltpu.make_async_copy(ref, ref, sem).wait()

    loads = []
    for m, w_hbm in enumerate((w_g_hbm, w_u_hbm, w_d_hbm)):
        for j in range(parts):
            load = pltpu.make_async_copy(
                w_hbm.at[:, pl.ds(j * part, part)], weights.at[m, j], w_sem.at[m, j]
            )
            load.start()
            loads.append(load)

    barrier = pltpu.get_barrier_semaphore()
    for k in range(1, groups):
        pl.semaphore_signal(barrier, inc=1, device_id={"dp": ahead(k)}, device_id_type=MESH)
    for j in range(1, parts):
        pl.semaphore_signal(
            barrier, inc=1, device_id={"expert": lax.rem(own + j, parts)}, device_id_type=MESH
        )
    pl.semaphore_wait(barrier, groups + parts - 2)

    for k in range(1, groups):
        to = ahead(k)
        for t in range(2):
            if t == 0:
                remote(send_t.at[to], recv_t.at[own, me], dp_send.at[0],
                       recv_sem.at[0, own, me], {"dp": to}).start()
    for k in range(1, groups):
        to = ahead(k)
        remote(send_s.at[to], recv_s.at[me], scale_send, scale_sem.at[me], {"dp": to}).start()
        remote(send_u.at[to], recv_u.at[own, me], dp_send.at[1],
               recv_sem.at[1, own, me], {"dp": to}).start()
    keeps = []
    for t in range(2):
        keep = pltpu.make_async_copy(sends[t].at[me], recvs[t].at[own, me], local_sem.at[t])
        keep.start()
        keeps.append(keep)
    recv_s[me] = send_s[me]

    def relay(t, k):
        s = behind(k)
        spot = recvs[t].at[own, s]
        if k == 0:
            source = sends[t].at[me]
        else:
            arrived(spot, recv_sem.at[t, own, s])
            source = spot
        for j in range(1, places):
            remote(source, spot, side_fwd.at[t], recv_sem.at[t, own, s],
                   {"expert": aside(j) * 2 + core}).start()
        remote(source, spot, pair_fwd.at[t], recv_sem.at[t, own, s], {"expert": partner}).start()

    def pass_on(t, k):
        s = behind(k)
        for j in range(1, places):
            part_of = aside(j) * 2 + core
            spot = recvs[t].at[part_of, s]
            arrived(spot, recv_sem.at[t, part_of, s])
            remote(spot, spot, pair_fwd.at[t], recv_sem.at[t, part_of, s],
                   {"expert": partner}).start()

    def finish(t):
        keeps[t].wait()
        for k in range(groups):
            s = behind(k)
            for j in range(places):
                part_of = aside(j) * 2 + (1 - core)
                arrived(recvs[t].at[part_of, s], recv_sem.at[t, part_of, s])

    def forward_unit(m, j):
        loads[m * parts + j].wait()
        block = recvs[m // 2][j].reshape(rows, part)
        value = contract_last(weights[m, j], block)
        if j == 0:
            pre[m] = value
        else:
            pre[m] = pre[m] + value

    units = [(m, j) for m in range(2) for j in range(parts)]
    steps = [(t, k) for t in range(2) for k in range(groups)]
    lag = 2
    begin = groups + lag
    for i in range(len(steps) + lag):
        if i < len(steps):
            relay(*steps[i])
        if i >= lag:
            pass_on(*steps[i - lag])
        if i == begin - 1:
            finish(0)
        if i >= begin - 1:
            share = -(-len(units) // max(1, len(steps) + lag - i))
            for _ in range(share):
                if units:
                    forward_unit(*units.pop(0))
    for unit in units:
        forward_unit(*unit)
    finish(1)
    for j in range(parts):
        forward_unit(2, j)

    for k in range(1, groups):
        arrived(recv_s.at[behind(k)], scale_sem.at[behind(k)])
    scale = jnp.transpose(recv_s[...].reshape(rows, 128).astype(jnp.float32))[0:1, :]
    tile = 32
    term[...] = jnp.zeros_like(term)

    @pl.loop(0, hid // tile)
    def _(step):
        at = pl.ds(pl.multiple_of(step * tile, tile), tile)
        gate, up, back = pre[0, at, :], pre[1, at, :], pre[2, at, :]
        sigma = jax.nn.sigmoid(gate)
        swish = gate * sigma
        slope = sigma * (1.0 + gate * (1.0 - sigma))
        act = (swish * up).astype(jnp.bfloat16).astype(jnp.float32)
        term[...] += jnp.broadcast_to(jnp.sum(act * back, axis=0, keepdims=True), term.shape)
        weighted = scale * back
        flipped[0, at, :] = (weighted * up * slope).astype(jnp.bfloat16)
        flipped[1, at, :] = (weighted * swish).astype(jnp.bfloat16)
        flipped[2, at, :] = (scale * act).astype(jnp.bfloat16)

    for j in range(1, parts):
        remote(term, term_recv.at[own], term_send, term_sem.at[own],
               {"expert": lax.rem(own + j, parts)}).start()
    for m in range(2):
        straight[m] = jnp.transpose(flipped[m].astype(jnp.float32)).astype(jnp.bfloat16)

    block_rows = min(rows, 256)

    def piece(which, lo):
        at = pl.ds(lo, block_rows)
        value = matmul(straight[0, at, :], weights[0, which])
        return value + matmul(straight[1, at, :], weights[1, which])

    chunk = block_rows // cap
    for j in list(range(1, places)) + [0]:
        there = aside(j) * 2
        for lo in range(0, rows, block_rows):
            value = piece(there + 1 - core, lo).astype(jnp.bfloat16)
            pair_send[j, pl.ds(lo // cap, chunk)] = value.reshape(chunk, cap, part)
        pair = remote(pair_send.at[j], pair_recv.at[j], pair_send_sem.at[j],
                      pair_recv_sem.at[j], {"expert": partner})
        pair.start()
        for lo in range(0, rows, block_rows):
            value = piece(there + core, lo)
            own_sum[pl.ds(lo // cap, chunk)] = value.reshape(chunk, cap, part)
        pair.wait_recv()
        if j == 0:
            continue
        for k in list(range(1, groups)) + [0]:
            to = ahead(k)
            both = own_sum[to] + pair_recv[j, to].astype(jnp.float32)
            side_send[j, to] = both.astype(jnp.bfloat16)
            remote(side_send.at[j, to], side_recv.at[j, to], side_send_sem.at[j],
                   side_recv_sem.at[j, to], {"expert": there + core}).start()

    stores = []

    def grad_unit(m, j):
        block = recvs[m // 2][j].reshape(rows, part)
        grads[m, j] = matmul(flipped[m], block).astype(jnp.bfloat16)
        store = pltpu.make_async_copy(
            grads.at[m, j], (out_g, out_u, out_d)[m].at[:, pl.ds(j * part, part)], g_sem.at[m, j]
        )
        store.start()
        stores.append(store)

    for j in range(1, parts):
        arrived(term_recv.at[lax.rem(own + j, parts)], term_sem.at[lax.rem(own + j, parts)])
    term_recv[own] = term[...]
    total = term_recv[0]
    for j in range(1, parts):
        total = total + term_recv[j]
    total_term[...] = total
    home_s[me] = total
    for k in range(1, groups):
        remote(total_term, home_s.at[me], back_send, back_recv.at[me], {"dp": ahead(k)}).start()

    units = [(m, j) for m in range(3) for j in range(parts)]
    order = list(range(1, groups)) + [0]
    for i, k in enumerate(order):
        for _ in range(-(-len(units) // (len(order) - i))):
            grad_unit(*units.pop(0))
        to = ahead(k)
        value = own_sum[to] + pair_recv[0, to].astype(jnp.float32)
        for j in range(1, places):
            arrived(side_recv.at[j, to], side_recv_sem.at[j, to])
            value = value + side_recv[j, to].astype(jnp.float32)
        if k == 0:
            home[me] = value.astype(jnp.bfloat16)
        else:
            out_send[to] = value.astype(jnp.bfloat16)
            remote(out_send.at[to], home.at[me], home_send, home_recv.at[me], {"dp": to}).start()

    for k in range(1, groups):
        s = behind(k)
        arrived(home.at[s], home_recv.at[s])
        arrived(home_s.at[s], back_recv.at[s])
    for store in stores:
        store.wait()
    arrived(recv_s.at[pl.ds(0, groups - 1)], scale_send)
    arrived(home.at[pl.ds(0, groups - 1)], home_send)
    arrived(home_s.at[pl.ds(0, groups - 1)], back_send)
    arrived(term_recv.at[pl.ds(0, parts - 1)], term_send)
    for t in range(2):
        arrived(recvs[t].at[0, pl.ds(0, groups - 1)], dp_send.at[t])
        arrived(recvs[t].at[pl.ds(0, places)], pair_fwd.at[t])
        if places > 1:
            arrived(recvs[t].at[pl.ds(0, places - 1)], side_fwd.at[t])
    for j in range(places):
        arrived(pair_send.at[j], pair_send_sem.at[j])
        if j:
            arrived(side_send.at[j], side_send_sem.at[j])


def exchange(send_t, send_u, send_s, w_gate, w_up, w_down, parts):
    groups, cap, part = send_t.shape
    rows = groups * cap
    hid, width = w_gate.shape
    places = parts // 2
    bf, f32 = jnp.bfloat16, jnp.float32
    dma = pltpu.SemaphoreType.DMA
    vmem = pl.BlockSpec(memory_space=pltpu.VMEM)
    hbm = pl.BlockSpec(memory_space=pl.ANY)
    grad = jax.ShapeDtypeStruct((hid, width), bf)
    return pl.pallas_call(
        functools.partial(kernel, groups, parts),
        out_shape=(
            jax.ShapeDtypeStruct((groups, cap, part), bf),
            jax.ShapeDtypeStruct((groups, 8, rows), f32),
            grad, grad, grad,
        ),
        in_specs=[vmem] * 3 + [hbm] * 3,
        out_specs=(vmem, vmem, hbm, hbm, hbm),
        scratch_shapes=[
            pltpu.VMEM((parts, groups, cap, part), bf),
            pltpu.VMEM((parts, groups, cap, part), bf),
            pltpu.VMEM((groups, cap, 128), bf),
            pltpu.VMEM((3, parts, hid, part), bf),
            pltpu.VMEM((3, hid, rows), f32),
            pltpu.VMEM((3, hid, rows), bf),
            pltpu.VMEM((2, rows, hid), bf),
            pltpu.VMEM((3, parts, hid, part), bf),
            pltpu.VMEM((8, rows), f32),
            pltpu.VMEM((parts, 8, rows), f32),
            pltpu.VMEM((8, rows), f32),
            pltpu.VMEM((places, groups, cap, part), bf),
            pltpu.VMEM((places, groups, cap, part), bf),
            pltpu.VMEM((places, groups, cap, part), bf),
            pltpu.VMEM((places, groups, cap, part), bf),
            pltpu.VMEM((groups, cap, part), f32),
            pltpu.VMEM((groups, cap, part), bf),
            dma((3, parts)), dma((3, parts)), dma((2,)), dma((2, parts, groups)),
            dma((groups,)), dma((2,)), dma((2,)), dma((2,)), dma,
            dma((places,)), dma((places,)), dma((places,)), dma((places, groups)),
            dma, dma((groups,)), dma, dma((parts,)), dma, dma((groups,)),
        ],
        compiler_params=pltpu.CompilerParams(
            collective_id=0, has_side_effects=True, vmem_limit_bytes=62 * 1024 * 1024
        ),
    )(send_t, send_u, send_s, w_gate, w_up, w_down)


def per_device(tokens, upstream, gates, expert_ids, w_gate, w_up, w_down):
    groups = lax.axis_size("dp")
    parts = lax.axis_size("expert")
    experts = groups * w_gate.shape[0]
    tok_rows, width = tokens.shape
    top = expert_ids.shape[1]
    cap = 2 * tok_rows * top // experts
    part = upstream.shape[1]
    rows = experts * cap
    own = lax.axis_index("expert")
    tok_part = lax.dynamic_slice_in_dim(tokens, own * part, part, axis=1)
    flat = expert_ids.reshape(-1)
    count = flat.shape[0]
    earlier = jnp.arange(count)[None, :] < jnp.arange(count)[:, None]
    same = flat[:, None] == flat[None, :]
    position = jnp.sum((earlier & same).astype(jnp.int32), axis=1)
    slot = (flat * cap + position).reshape(tok_rows, top)
    hit = slot[None, :, :] == jnp.arange(rows, dtype=jnp.int32)[:, None, None]
    pick = jnp.sum(hit.astype(jnp.float32), axis=2).astype(jnp.bfloat16)
    scale = jnp.sum(jnp.where(hit, gates.astype(jnp.float32)[None], 0.0), axis=(1, 2))
    send_t = matmul(pick, tok_part).astype(jnp.bfloat16).reshape(groups, cap, part)
    send_u = matmul(pick, upstream).astype(jnp.bfloat16).reshape(groups, cap, part)
    send_s = jnp.broadcast_to(scale[:, None], (rows, 128)).astype(jnp.bfloat16)
    home, home_s, grad_gate, grad_up, grad_down = exchange(
        send_t, send_u, send_s.reshape(groups, cap, 128), w_gate[0], w_up[0], w_down[0], parts
    )
    grad_x = contract_first(pick, home.reshape(rows, part)).astype(jnp.bfloat16)
    terms = home_s[:, 0, :].reshape(groups, groups, cap)
    terms = lax.dynamic_index_in_dim(terms, lax.axis_index("dp"), 1, keepdims=False).reshape(rows)
    grad_gates = jnp.sum(jnp.where(hit, terms[:, None, None], 0.0), axis=0)
    return (grad_x, grad_gates, grad_gate[None], grad_up[None], grad_down[None])


def solution(mesh):
    in_specs = (
        P("dp", None),
        P("dp", "expert"),
        P("dp", None),
        P("dp", None),
        P("dp", "expert", None),
        P("dp", "expert", None),
        P("dp", "expert", None),
    )
    out_specs = (
        P("dp", "expert"),
        P("dp", None),
        P("dp", "expert", None),
        P("dp", "expert", None),
        P("dp", "expert", None),
    )
    return jax.shard_map(
        per_device, mesh=mesh, in_specs=in_specs, out_specs=out_specs, check_vma=False
    )
```

profile of v0, /device:TPU:0, one launch (start us, length us, event | category | flops | bytes accessed | tf_op | source)
XLA Modules:
  0.0 125.4 jit_solution(10192943422890829041)
XLA Ops:
  0.6 0.0 copy-start
  0.7 0.7 convert_element_type.34
  1.4 0.8 copy.22
  2.2 0.1 eq.28
  2.3 0.2 convert_reduce_fusion.1
  2.5 0.1 reduce_sum.39
  2.7 0.1 copy.23
  2.7 0.7 multiply_add_fusion
  3.4 0.2 select_reduce_fusion.1
  3.6 0.1 convert_element_type.36
  3.7 0.8 broadcast_in_dim.45.send_s
  4.5 0.0 copy-done
  4.5 1.4 %convolution_convert_fusion.1 = bf16[512,1024]{1,0:T(8,128)(2,1)} fusion(bf16[128,4096]{1,0:T(8,128)(2,1)S(1)} %copy-done, s32[]{:T(128)S(6)} %select_n.15, bf16[512,128]{1,0:T(8,128)(2,1)S(1)} %get-tuple-element.16), kind=kOutput, calls=%fused_computation.1 | convolution fusion | flops 134742016 | bytes 1441796 | tf_op jit(solution)/shard_map/dot_general | solution.py:26
  5.9 2.3 %convolution_convert_fusion = bf16[512,1024]{1,0:T(8,128)(2,1)} fusion(bf16[128,1024]{1,0:T(8,128)(2,1)} %param.8, bf16[512,128]{1,0:T(8,128)(2,1)S(1)} %get-tuple-element.16), kind=kOutput, calls=%fused_computation | convolution fusion | flops 134742016 | bytes 1441792 | tf_op jit(solution)/shard_map/dot_general | solution.py:26
  8.2 104.3 %shard_map.110 = (bf16[8,64,1024]{2,1,0:T(8,128)(2,1)}, f32[8,8,512]{2,1,0:T(8,128)}, bf16[384,4096]{1,0:T(8,128)(2,1)}, bf16[384,4096]{1,0:T(8,128)(2,1)}, bf16[384,4096]{1,0:T(8,128)(2,1)}) custom-call(bf16[8,64,1024]{2,1,0:T(8,128)(2,1)} %bitcast.14, bf16[8,64,1024]{2,1,0:T(8,128)(2,1)} %bitcast.15, bf16[8,64,128]{2,1,0:T(8,128)(2,1)} %broadcast_in_dim.45.send_s, ...), custom_call_target="tpu_custom_call" | custom-call | tf_op jit(solution)/shard_map/pallas_call | solution.py:296
  112.5 2.3 %convolution_convert_fusion.2 = bf16[128,1024]{1,0:T(8,128)(2,1)} fusion(bf16[512,1024]{1,0:T(8,128)(2,1)} %bitcast.22, bf16[512,128]{1,0:T(8,128)(2,1)S(1)} %get-tuple-element.16), kind=kOutput, calls=%fused_computation.2 | convolution fusion | flops 134348800 | bytes 1441792 | tf_op jit(solution)/shard_map/dot_general | solution.py:20
  114.8 0.9 slice_reduce_fusion
  115.7 0.1 reshape_squeeze.3
  115.8 0.1 broadcast_in_dim.46
  115.9 0.7 select_reduce_fusion
  116.6 0.0 copy-start.2
  116.6 4.1 %copy.27 = bf16[1,384,4096]{2,1,0:T(8,128)(2,1)} copy(bf16[1,384,4096]{2,1,0:T(8,128)(2,1)} %bitcast.18) | data formatting | bytes 6291456
  120.7 0.0 copy-done.2
  120.7 0.0 copy-start.1
  120.7 1.7 %copy.28 = bf16[1,384,4096]{2,1,0:T(8,128)(2,1)} copy(bf16[1,384,4096]{2,1,0:T(8,128)(2,1)S(1)} %bitcast.17) | data formatting | bytes 6291456
  122.3 1.4 %copy-done.1 = bf16[384,4096]{1,0:T(8,128)(2,1)S(1)} copy-done((bf16[384,4096]{1,0:T(8,128)(2,1)S(1)}, bf16[384,4096]{1,0:T(8,128)(2,1)}, u32[]{:S(2)}) %copy-start.1) | copy-done | bytes 3145752
  123.7 1.7 %copy.29 = bf16[1,384,4096]{2,1,0:T(8,128)(2,1)} copy(bf16[1,384,4096]{2,1,0:T(8,128)(2,1)S(1)} %bitcast.16) | data formatting | bytes 6291456
  (1 shorter events, 0.0 us)
Async XLA Ops:
  0.6 3.8 %copy-start = (bf16[128,4096]{1,0:T(8,128)(2,1)S(1)}, bf16[128,4096]{1,0:T(8,128)(2,1)}, u32[]{:S(2)}) copy-start(bf16[128,4096]{1,0:T(8,128)(2,1)} %param.7) | copy-start | bytes 3145732
  116.6 4.1 %copy-start.2 = (bf16[384,4096]{1,0:T(8,128)(2,1)S(1)}, bf16[384,4096]{1,0:T(8,128)(2,1)}, u32[]{:S(2)}) copy-start(bf16[384,4096]{1,0:T(8,128)(2,1)} %get-tuple-element.13) | copy-start | bytes 9437188
  120.7 3.0 %copy-start.1 = (bf16[384,4096]{1,0:T(8,128)(2,1)S(1)}, bf16[384,4096]{1,0:T(8,128)(2,1)}, u32[]{:S(2)}) copy-start(bf16[384,4096]{1,0:T(8,128)(2,1)} %get-tuple-element.14) | copy-start | bytes 9437188
where the time goes:
time: 127 us; the launch traced here: 125 us
  Pallas kernels  104 us (82%)
  local copies, waits for them, and re-layouts  11.9 us (9%)
  matrix products  6 us (5%)
  other arithmetic  2.52 us (2%)
    pallas_call x1, Pallas kernels, exchange(): pl.pallas_call(functools.partial(kernel, groups, parts), out_shape=(jax.S...  104 us
    unnamed x10, local copies, waits for them, and re-layouts  9.54 us
    dot_general x2, matrix products, matmul(): return jnp.dot(left, right, preferred_element_type=jnp.float32)  3.73 us

commit v1 on v0

v1 whole, which is shorter than its diff:
```python
import functools

import jax
import jax.numpy as jnp
from jax import lax
from jax.experimental import pallas as pl
from jax.experimental.pallas import tpu as pltpu
from jax.sharding import PartitionSpec as P

MESH = pltpu.DeviceIdType.MESH if hasattr(pltpu, "DeviceIdType") else pl.DeviceIdType.MESH
LANES = 128


def contract_last(left, right):
    return lax.dot_general(
        left, right, (((1,), (1,)), ((), ())), preferred_element_type=jnp.float32
    )


def contract_first(left, right):
    return lax.dot_general(
        left, right, (((0,), (0,)), ((), ())), preferred_element_type=jnp.float32
    )


def matmul(left, right):
    return jnp.dot(left, right, preferred_element_type=jnp.float32)


def kernel(
    groups, parts,
    ids_ref, gates_ref, tok_hbm, ups_hbm, w_g_hbm, w_u_hbm, w_d_hbm,
    gx_out, gg_out, out_g, out_u, out_d,
    tok, ups, pick, send_t, send_u, recv_t, recv_u, weights, pre, flipped, straight,
    scale_send, scale_recv, scale_row, term, term_recv, total, home_s,
    pair_send, pair_recv, side_send, side_recv, own_sum, out_send, home, gx_acc,
    load_sem, w_sem, recv_sem, scale_sem, dp_near, dp_far, dp_up, pair_fwd, side_fwd,
    scale_out, pair_send_sem, pair_recv_sem, side_send_sem, side_recv_sem,
    home_send, home_recv, term_send, term_sem, back_send, back_recv,
):
    me, own = lax.axis_index("dp"), lax.axis_index("expert")
    core, place = lax.rem(own, 2), lax.div(own, 2)
    places = parts // 2
    partner = place * 2 + (1 - core)
    cap, part = send_u.shape[1:]
    top, count = ids_ref.shape
    rows = groups * cap
    hid = weights.shape[2]
    near = groups // 2
    per_tile = LANES // cap
    recvs = (recv_t, recv_u)
    quarter = (groups - near) // 2
    chunks = [(0, near), (near, quarter), (near + quarter, groups - near - quarter)]
    bf, f32 = jnp.bfloat16, jnp.float32

    def ahead(k):
        spot = me
        for bit in [1 << b for b in range(groups.bit_length()) if k >> b & 1]:
            spot = spot + bit * (1 - 2 * lax.rem(lax.div(me, bit), 2))
        return spot

    def aside(j):
        return lax.rem(place + j, places) * 2 + core

    def columns(r):
        j, other = divmod(r, 2)
        spot = lax.rem(place + j, places) * 2 + (1 - core if other else core)
        return pl.ds(pl.multiple_of(spot * part, part), part)

    def remote(src, dst, send_sem, sem, target):
        return pltpu.make_async_remote_copy(
            src_ref=src, dst_ref=dst, send_sem=send_sem, recv_sem=sem,
            device_id=target, device_id_type=MESH,
        )

    def arrived(ref, sem):
        pltpu.make_async_copy(ref, ref, sem).wait()

    barrier = pltpu.get_barrier_semaphore()
    for k in range(1, groups):
        pl.semaphore_signal(barrier, inc=1, device_id={"dp": ahead(k)}, device_id_type=MESH)
    for j in range(1, parts):
        pl.semaphore_signal(
            barrier, inc=1, device_id={"expert": lax.rem(own + j, parts)}, device_id_type=MESH
        )

    feeds = [
        pltpu.make_async_copy(tok_hbm.at[:, columns(2 * j)], tok.at[j], load_sem.at[j])
        for j in range(places)
    ]
    feeds.append(pltpu.make_async_copy(ups_hbm, ups, load_sem.at[places]))
    for feed in feeds:
        feed.start()
    step_of = lax.broadcasted_iota(jnp.int32, (groups, count), 0)
    expert = jnp.zeros((groups, count), jnp.int32)
    for k in range(groups):
        expert = jnp.where(step_of == k, ahead(k), expert)
    named = [ids_ref[j : j + 1, :] == expert for j in range(top)]
    member = jnp.zeros((groups, count), f32)
    weight = jnp.zeros((groups, count), f32)
    gates = gates_ref[...].astype(f32)
    for j in range(top):
        member = jnp.where(named[j], 1.0, member)
        weight = jnp.where(named[j], gates[j : j + 1, :], weight)
    earlier = (
        lax.broadcasted_iota(jnp.int32, (count, count), 0)
        < lax.broadcasted_iota(jnp.int32, (count, count), 1)
    )
    before = matmul(member.astype(bf), jnp.where(earlier, 1.0, 0.0).astype(bf))
    place_of = jnp.where(member > 0.5, before, -1.0)
    slot_of = lax.broadcasted_iota(jnp.int32, (cap, count), 0).astype(f32)
    for k in range(groups):
        hit = place_of[k : k + 1, :] == slot_of
        pick[pl.ds(k * cap, cap), :] = jnp.where(hit, 1.0, 0.0).astype(bf)

    lane = lax.broadcasted_iota(jnp.int32, (groups, rows), 1)
    first = lax.broadcasted_iota(jnp.int32, (groups, rows), 0) * cap
    own_block = (lane >= first) & (lane < first + cap)
    scales = contract_last(weight.astype(bf), pick[...])
    scales = jnp.sum(jnp.where(own_block, scales, 0.0), axis=0, keepdims=True)
    for i in range(rows // LANES):
        scale_send[i] = jnp.broadcast_to(scales[:, i * LANES : (i + 1) * LANES], (8, LANES))

    block_steps = per_tile

    def gather(b):
        at = pl.ds(b * LANES, LANES)
        steps = range(b * block_steps, (b + 1) * block_steps)
        for j in range(places if steps[0] < near else 1):
            value = matmul(pick[at, :], tok[j]).astype(bf).reshape(block_steps, cap, part)
            for i, k in enumerate(steps):
                if k:
                    send_t[j, k] = value[i]
                else:
                    recv_t[2 * j, 0] = value[i]
        value = matmul(pick[at, :], ups[...]).astype(bf).reshape(block_steps, cap, part)
        for i, k in enumerate(steps):
            if k:
                send_u[k] = value[i]
            else:
                recv_u[0, 0] = value[i]

    def dispatch(b):
        for k in range(b * block_steps, (b + 1) * block_steps):
            if k == 0:
                continue
            to = {"dp": ahead(k)}
            remote(scale_send.at[k // per_tile], scale_recv.at[k], scale_out, scale_sem.at[k],
                   to).start()
            if k < near:
                for j in range(places):
                    remote(send_t.at[j, k], recv_t.at[2 * j, k], dp_near,
                           recv_sem.at[0, 2 * j, k], to).start()
            else:
                remote(send_t.at[0, k], recv_t.at[0, k], dp_far, recv_sem.at[0, 0, k], to).start()
            remote(send_u.at[k], recv_u.at[0, k], dp_up, recv_sem.at[1, 0, k], to).start()

    with jax.named_scope("feedwait"):
        for feed in feeds:
            feed.wait()
    blocks = rows // LANES
    near_blocks = near // block_steps
    order = list(range(1, near_blocks)) + [0] + list(range(near_blocks, blocks))
    with jax.named_scope("gather0"):
        gather(order[0])
    with jax.named_scope("A_barrier"):
        pl.semaphore_wait(barrier, groups + parts - 2)
    dispatch(order[0])
    for b in order[1:]:
        gather(b)
        dispatch(b)

    loads = []
    for m, w_hbm in enumerate((w_g_hbm, w_u_hbm, w_d_hbm)):
        for r in range(parts):
            load = pltpu.make_async_copy(w_hbm.at[:, columns(r)], weights.at[m, r], w_sem.at[m, r])
            load.start()
            loads.append(load)

    def relay(t, k):
        if t == 0 and k < near:
            for j in range(places):
                spot = recv_t.at[2 * j, k]
                if k:
                    arrived(spot, recv_sem.at[0, 2 * j, k])
                remote(spot, recv_t.at[2 * j + 1, k], pair_fwd.at[0],
                       recv_sem.at[0, 2 * j + 1, k], {"expert": partner}).start()
            return
        spot = recvs[t].at[0, k]
        if k:
            arrived(spot, recv_sem.at[t, 0, k])
        for j in range(1, places):
            r = 2 * (places - j)
            remote(spot, recvs[t].at[r, k], side_fwd.at[t], recv_sem.at[t, r, k],
                   {"expert": aside(j)}).start()
        remote(spot, recvs[t].at[1, k], pair_fwd.at[t], recv_sem.at[t, 1, k],
               {"expert": partner}).start()

    def pass_on(t, k):
        if t == 0 and k < near:
            return
        for j in range(1, places):
            spot = recvs[t].at[2 * j, k]
            arrived(spot, recv_sem.at[t, 2 * j, k])
            remote(spot, recvs[t].at[2 * j + 1, k], pair_fwd.at[t],
                   recv_sem.at[t, 2 * j + 1, k], {"expert": partner}).start()

    def finish(c):
        lo, n = chunks[c]
        for t in range(2):
            for k in range(lo, lo + n):
                for j in range(places):
                    arrived(recvs[t].at[2 * j + 1, k], recv_sem.at[t, 2 * j + 1, k])

    def forward_unit(c, m, r):
        lo, n = chunks[c]
        if c == 0:
            loads[m * parts + r].wait()
        at = pl.ds(lo * cap, n * cap)
        block = recvs[m // 2][r, pl.ds(lo, n)].reshape(n * cap, part)
        value = contract_last(weights[m, r], block)
        if r == 0:
            pre[m, :, at] = value
        else:
            pre[m, :, at] = pre[m, :, at] + value

    def mine(k, shape):
        spot = lax.broadcasted_iota(jnp.int32, shape, 1)
        low = k % per_tile * cap
        return (spot >= low) & (spot < low + cap)

    def merge_tile(i, source):
        value = jnp.zeros((8, LANES), f32)
        for k in range(i * per_tile, (i + 1) * per_tile):
            value = jnp.where(mine(k, (8, LANES)), source(k), value)
        return value

    tile = 32

    def elementwise(c):
        lo, n = chunks[c]
        at = pl.ds(lo * cap, n * cap)
        for k in range(max(lo, 1), lo + n):
            arrived(scale_recv.at[k], scale_sem.at[k])
        for i in range(lo // per_tile, (lo + n) // per_tile):
            scale_row[:, pl.ds(i * LANES, LANES)] = merge_tile(
                i, lambda k: scale_recv[k] if k else scale_send[0]
            )
        scale = scale_row[0:1, at]
        term[:, at] = jnp.zeros((8, n * cap), f32)

        @pl.loop(0, hid // tile)
        def _(step):
            spot = pl.ds(pl.multiple_of(step * tile, tile), tile)
            gate, up, back = pre[0, spot, at], pre[1, spot, at], pre[2, spot, at]
            sigma = jax.nn.sigmoid(gate)
            swish = gate * sigma
            slope = sigma * (1.0 + gate * (1.0 - sigma))
            act = (swish * up).astype(bf).astype(f32)
            term[:, at] += jnp.broadcast_to(
                jnp.sum(act * back, axis=0, keepdims=True), (8, n * cap)
            )
            weighted = scale * back
            flipped[0, spot, at] = (weighted * up * slope).astype(bf)
            flipped[1, spot, at] = (weighted * swish).astype(bf)
            flipped[2, spot, at] = (scale * act).astype(bf)

    def straighten(c):
        lo, n = chunks[c]
        at = pl.ds(lo * cap, n * cap)
        for m in range(2):
            straight[m, at, :] = jnp.transpose(flipped[m, :, at].astype(f32)).astype(bf)

    def piece(c, r):
        lo, n = chunks[c]
        at = pl.ds(lo * cap, n * cap)
        value = matmul(straight[0, at, :], weights[0, r])
        value = value + matmul(straight[1, at, :], weights[1, r])
        return value.reshape(n, cap, part)

    def pair(c, j):
        lo, n = chunks[c]
        at = pl.ds(lo, n)
        return remote(pair_send.at[j, at], pair_recv.at[j, at], pair_send_sem.at[j, c],
                      pair_recv_sem.at[j, c], {"expert": partner})

    def partial_other(c, j):
        lo, n = chunks[c]
        pair_send[j, pl.ds(lo, n)] = piece(c, 2 * j + 1).astype(bf)
        pair(c, j).start()

    def partial_own(c, j):
        lo, n = chunks[c]
        own_sum[j, pl.ds(lo, n)] = piece(c, 2 * j)

    def sideways(c, j, piece_of=0, pieces=1):
        lo, n = chunks[c]
        if piece_of == 0:
            pair(c, j).wait_recv()
        share = n // pieces
        for k in reversed(range(lo + n - (piece_of + 1) * share, lo + n - piece_of * share)):
            both = own_sum[j, k] + pair_recv[j, k].astype(f32)
            side_send[j, k] = both.astype(bf)
            remote(side_send.at[j, k], side_recv.at[j, k], side_send_sem.at[j],
                   side_recv_sem.at[j, k], {"expert": aside(j)}).start()

    def homeward(c, k):
        lo, n = chunks[c]
        if k == lo + n - 1:
            pair(c, 0).wait_recv()
        value = own_sum[0, k] + pair_recv[0, k].astype(f32)
        for j in range(1, places):
            arrived(side_recv.at[j, k], side_recv_sem.at[j, k])
            value = value + side_recv[j, k].astype(f32)
        if k == 0:
            home[0] = value.astype(bf)
        else:
            out_send[k] = value.astype(bf)
            remote(out_send.at[k], home.at[k], home_send, home_recv.at[k],
                   {"dp": ahead(k)}).start()

    def collect(c):
        lo, n = chunks[c]
        for k in range(max(lo, 1), lo + n):
            arrived(home.at[k], home_recv.at[k])
        value = contract_first(
            pick[pl.ds(lo * cap, n * cap), :], home[pl.ds(lo, n)].reshape(n * cap, part)
        )
        if c == 0:
            gx_acc[...] = value
        elif c < len(chunks) - 1:
            gx_acc[...] = gx_acc[...] + value
        else:
            gx_out[...] = (gx_acc[...] + value).astype(bf)

    def grad_unit(m, r):
        block = recvs[m // 2][r].reshape(rows, part)
        (out_g, out_u, out_d)[m][:, columns(r)] = matmul(flipped[m], block).astype(bf)

    def first_half(c):
        tasks = [functools.partial(forward_unit, c, m, r) for m in range(3) for r in range(parts)]
        tasks.append(functools.partial(elementwise, c))
        tasks.append(functools.partial(straighten, c))
        return tasks

    def second_half(c):
        tasks = []
        for j in list(range(1, places)) + [0]:
            tasks.append(functools.partial(partial_other, c, j))
            tasks.append(functools.partial(partial_own, c, j))
        return tasks

    def side_half(c):
        return [functools.partial(sideways, c, j) for j in range(1, places)]

    def side_part(c, piece_of):
        for j in range(1, places):
            sideways(c, j, piece_of, 2)

    def last_half(c):
        lo, n = chunks[c]
        return [functools.partial(homeward, c, k) for k in reversed(range(lo, lo + n))]

    def run(tasks, number):
        for _ in range(min(number, len(tasks))):
            tasks.pop(0)()

    waiting = []

    def events(c, tasks, lag):
        lo, n = chunks[c]
        steps = [(t, k) for k in range(lo, lo + n) for t in range(2)]
        for i, step in enumerate(steps):
            with jax.named_scope("relay%d_t%d_k%d" % (c, step[0], step[1])):
                relay(*step)
            waiting.append(step)
            if len(waiting) > lag:
                with jax.named_scope("pass%d" % c):
                    pass_on(*waiting.pop(0))
            if tasks:
                with jax.named_scope("work%d_%d" % (c, i)):
                    run(tasks, -(-len(tasks) // (len(steps) - i)))

    def settle(c):
        with jax.named_scope("settle%d" % c):
            while waiting and waiting[0][1] < chunks[c][0] + chunks[c][1]:
                pass_on(*waiting.pop(0))
            finish(c)

    never = 2 * groups
    events(0, [], 4)
    events(1, [], never)
    settle(0)
    events(2, first_half(0) + second_half(0), never)
    settle(1)
    with jax.named_scope("work1"):
        for task in first_half(1) + second_half(1) + side_half(1):
            task()
        side_part(0, 0)
    settle(2)
    with jax.named_scope("first2"):
        for task in first_half(2):
            task()
    for j in range(1, parts):
        remote(term, term_recv.at[own], term_send, term_sem.at[own],
               {"expert": lax.rem(own + j, parts)}).start()
    with jax.named_scope("second2"):
        for task in second_half(2) + side_half(2):
            task()
    with jax.named_scope("homeward1"):
        for task in last_half(1):
            task()
    side_part(0, 1)
    units = [functools.partial(grad_unit, m, r) for m in range(3) for r in range(parts)]
    with jax.named_scope("grads"):
        run(units, 1)
    with jax.named_scope("termwait"):
        for j in range(1, parts):
            arrived(term_recv.at[lax.rem(own + j, parts)], term_sem.at[lax.rem(own + j, parts)])
    term_recv[own] = term[...]
    whole = term_recv[0]
    for j in range(1, parts):
        whole = whole + term_recv[j]
    for i in range(rows // LANES):
        total[i] = whole[:, i * LANES : (i + 1) * LANES]
    for k in range(1, groups):
        remote(total.at[k // per_tile], home_s.at[k], back_send, back_recv.at[k],
               {"dp": ahead(k)}).start()
    with jax.named_scope("grads"):
        run(units, 1)
    with jax.named_scope("homeward2"):
        for task in last_half(2):
            task()
    with jax.named_scope("grads"):
        run(units, 2)
    for task in last_half(0):
        with jax.named_scope("homeward0"):
            task()
        with jax.named_scope("grads"):
            run(units, 1)
    with jax.named_scope("grads"):
        run(units, len(units))
    with jax.named_scope("collect0"):
        collect(0)
    with jax.named_scope("collect1"):
        collect(1)

    with jax.named_scope("gates"):
        for k in range(1, groups):
            arrived(home_s.at[k], back_recv.at[k])
        line = jnp.concatenate(
            [
                merge_tile(i, lambda k: home_s[k] if k else total[0])[0:1, :]
                for i in range(rows // LANES)
            ],
            axis=1,
        )
        spread = jnp.where(own_block, jnp.broadcast_to(line, (groups, rows)), 0.0)
        high = spread.astype(bf)
        rest = spread - high.astype(f32)
        mid = rest.astype(bf)
        low = (rest - mid.astype(f32)).astype(bf)
        picked = pick[...]
        found = matmul(high, picked) + matmul(mid, picked) + matmul(low, picked)
        for j in range(top):
            gg_out[j : j + 1, :] = jnp.sum(
                jnp.where(ids_ref[j : j + 1, :] == expert, found, 0.0), axis=0, keepdims=True
            )
    with jax.named_scope("collect2"):
        collect(2)

    arrived(scale_recv.at[pl.ds(1, groups - 1)], scale_out)
    arrived(home.at[pl.ds(0, groups - 1)], home_send)
    arrived(home_s.at[pl.ds(1, groups - 1)], back_send)
    arrived(term_recv.at[pl.ds(0, parts - 1)], term_send)
    arrived(recv_t.at[pl.ds(0, places), pl.ds(0, near - 1)], dp_near)
    arrived(recv_t.at[0, pl.ds(0, groups - near)], dp_far)
    arrived(recv_u.at[0, pl.ds(0, groups - 1)], dp_up)
    for t in range(2):
        arrived(recvs[t].at[pl.ds(0, places)], pair_fwd.at[t])
    if places > 1:
        arrived(recv_t.at[pl.ds(0, places - 1), pl.ds(0, groups - near)], side_fwd.at[0])
        arrived(recv_u.at[pl.ds(0, places - 1)], side_fwd.at[1])
    for j in range(places):
        for c in range(len(chunks)):
            pair(c, j).wait_send()
        if j:
            arrived(side_send.at[j], side_send_sem.at[j])


def put_out(*refs):
    number = len(refs) // 2
    sources, targets, sems = refs[:number], refs[number : 2 * number], refs[2 * number]
    copies = [
        pltpu.make_async_copy(sources[i], targets[i], sems.at[i]) for i in range(number)
    ]
    for copy in copies:
        copy.start()
    for copy in copies:
        copy.wait()


def exchange(ids, gates, tokens, upstream, w_gate, w_up, w_down, groups, parts, cap):
    top, count = ids.shape
    hid, width = w_gate.shape
    part = upstream.shape[1]
    rows = groups * cap
    places = parts // 2
    near = groups // 2
    bf, f32 = jnp.bfloat16, jnp.float32
    dma = pltpu.SemaphoreType.DMA
    vmem = pl.BlockSpec(memory_space=pltpu.VMEM)
    hbm = pl.BlockSpec(memory_space=pl.ANY)
    shapes = [((count, part), bf), ((top, count), f32)] + [((hid, width), bf)] * 3
    results = pl.pallas_call(
        functools.partial(kernel, groups, parts),
        out_shape=tuple(OUT(shape, kind) for shape, kind in shapes),
        in_specs=[vmem] * 2 + [hbm] * 5,
        out_specs=(vmem,) * 5,
        scratch_shapes=[
            pltpu.VMEM((places, count, part), bf),
            pltpu.VMEM((count, part), bf),
            pltpu.VMEM((rows, count), bf),
            pltpu.VMEM((places, groups, cap, part), bf),
            pltpu.VMEM((groups, cap, part), bf),
            pltpu.VMEM((parts, groups, cap, part), bf),
            pltpu.VMEM((parts, groups, cap, part), bf),
            pltpu.VMEM((3, parts, hid, part), bf),
            pltpu.VMEM((3, hid, rows), f32),
            pltpu.VMEM((3, hid, rows), bf),
            pltpu.VMEM((2, rows, hid), bf),
            pltpu.VMEM((rows // LANES, 8, LANES), f32),
            pltpu.VMEM((groups, 8, LANES), f32),
            pltpu.VMEM((8, rows), f32),
            pltpu.VMEM((8, rows), f32),
            pltpu.VMEM((parts, 8, rows), f32),
            pltpu.VMEM((rows // LANES, 8, LANES), f32),
            pltpu.VMEM((groups, 8, LANES), f32),
            pltpu.VMEM((places, groups, cap, part), bf),
            pltpu.VMEM((places, groups, cap, part), bf),
            pltpu.VMEM((places, groups, cap, part), bf),
            pltpu.VMEM((places, groups, cap, part), bf),
            pltpu.VMEM((places, groups, cap, part), f32),
            pltpu.VMEM((groups, cap, part), bf),
            pltpu.VMEM((groups, cap, part), bf),
            pltpu.VMEM((count, part), f32),
            dma((places + 1,)), dma((3, parts)), dma((2, parts, groups)), dma((groups,)),
            dma, dma, dma, dma((2,)), dma((2,)),
            dma, dma((places, 3)), dma((places, 3)), dma((places,)), dma((places, groups)),
            dma, dma((groups,)), dma, dma((parts,)), dma, dma((groups,)),
        ],
        compiler_params=pltpu.CompilerParams(
            collective_id=0, has_side_effects=True, vmem_limit_bytes=50 * 1024 * 1024
        ),
    )(ids, gates, tokens, upstream, w_gate, w_up, w_down)
    return pl.pallas_call(
        put_out,
        out_shape=tuple(jax.ShapeDtypeStruct(shape, kind) for shape, kind in shapes),
        in_specs=[vmem] * 5,
        out_specs=(hbm,) * 5,
        scratch_shapes=[dma((5,))],
        compiler_params=pltpu.CompilerParams(vmem_limit_bytes=2 * 1024 * 1024),
    )(*results)


def OUT(shape, kind):
    return pltpu.VMEM(shape, kind)


def per_device(tokens, upstream, gates, expert_ids, w_gate, w_up, w_down):
    groups = lax.axis_size("dp")
    parts = lax.axis_size("expert")
    experts = groups * w_gate.shape[0]
    cap = 2 * tokens.shape[0] * expert_ids.shape[1] // experts
    grad_x, grad_gates, grad_gate, grad_up, grad_down = exchange(
        expert_ids.T, gates.T, tokens, upstream, w_gate[0], w_up[0], w_down[0],
        groups, parts, cap,
    )
    return (grad_x, grad_gates.T, grad_gate[None], grad_up[None], grad_down[None])


def solution(mesh):
    in_specs = (
        P("dp", None),
        P("dp", "expert"),
        P("dp", None),
        P("dp", None),
        P("dp", "expert", None),
        P("dp", "expert", None),
        P("dp", "expert", None),
    )
    out_specs = (
        P("dp", "expert"),
        P("dp", None),
        P("dp", "expert", None),
        P("dp", "expert", None),
        P("dp", "expert", None),
    )
    return jax.shard_map(
        per_device, mesh=mesh, in_specs=in_specs, out_specs=out_specs, check_vma=False
    )
```

time: 127 us -> 103 us (0.81); the launches traced: 125 us -> 103 us
  local copies, waits for them, and re-layouts: 11.9 us -> 0 us
  matrix products: 6 us -> 0 us
  other arithmetic: 2.52 us -> 0 us
    unnamed x10 -> x0, local copies, waits for them, and re-layouts: 9.54 us -> none
    dot_general x3 -> x0, matrix products: 6 us -> none  [the longest x2 3.73 us: matmul(): return jnp.dot(left, right, preferred_element_type=jnp.float32)]
    pallas_call x1 -> x2, Pallas kernels: 104 us -> 103 us  [the longest x1 98.6 us: exchange(): pl.pallas_call(functools.partial(kernel, groups, parts), out_shape=tuple(...]
where the time goes in v1:
time: 103 us
  Pallas kernels  103 us (100%)
    pallas_call x1, Pallas kernels, exchange(): pl.pallas_call(functools.partial(kernel, groups, parts), out_shape=tuple(...  98.6 us
    pallas_call x1, Pallas kernels, exchange(): pl.pallas_call(put_out, out_shape=tuple((jax.ShapeDtypeStruct(shape, kind...  3.87 us

profile of v1, /device:TPU:0, one launch (start us, length us, event | category | flops | bytes accessed | tf_op | source)
XLA Modules:
  0.0 103.3 jit_solution(14761659285866447811)
XLA Ops:
  0.6 98.6 %shard_map.110 = (bf16[128,1024]{1,0:T(8,128)(2,1)S(1)}, f32[2,128]{1,0:T(2,128)S(1)}, bf16[384,4096]{1,0:T(8,128)(2,1)S(1)}, bf16[384,4096]{1,0:T(8,128)(2,1)S(1)}, bf16[384,4096]{1,0:T(8,128)(2,1)S(1)}) custom-call(s32[2,128]{1,0:T(2,128)} %bitcast.12, bf16[2,128]{1,0:T(2,128)(2,1)} %bitcast.13, bf16[128,4096]{1,0:T(8,128)(2,1)} %tok_hbm.1, ...), custom_call_target="tpu_custom_call" | custom-call | tf_op jit(solution)/shard_map/pallas_call | solution.py:515
  99.3 3.9 %shard_map.111 = (bf16[128,1024]{1,0:T(8,128)(2,1)}, f32[2,128]{1,0:T(2,128)}, bf16[384,4096]{1,0:T(8,128)(2,1)}, bf16[384,4096]{1,0:T(8,128)(2,1)}, bf16[384,4096]{1,0:T(8,128)(2,1)}) custom-call(bf16[128,1024]{1,0:T(8,128)(2,1)S(1)} %get-tuple-element.15.refs_0_, f32[2,128]{1,0:T(2,128)S(1)} %get-tuple-element.16.refs_1_, ...), custom_call_target="tpu_custom_call" | custom-call | tf_op jit(solution)/shard_map/pallas_call | solution.py:556
